TPU v7x, 512 devices: a whole 4x4x16 slice. The times are simulated.
512 devices in a mesh: tile: 32 (over y, x, core), depth: 16 (over z).
Axes of the slice: x: 4, y: 4, z: 16, core: 2. Of those that a mesh axis runs over, the one named last changes fastest.
Arguments:
- features: bfloat16 [16, 8192, 128], P('depth', 'tile'), may hold values from -4 to 4
- logits: float32 [16, 8192], P('depth', 'tile'), may hold values from -2.75 to 5.5
- geometry: float32 [2, 16, 5, 8192], P(None, 'depth', None, 'tile'), may hold values from -0.6 to 32, as said below
- dest_slot: int32 [2, 16, 8192], P(None, 'depth', 'tile'), may hold values from -1 to 8191, as said below
- target: bfloat16 [2, 64, 128, 1024], P(None, 'tile'), may hold values from -3 to 3
Outputs:
- images: bfloat16 [2, 64, 128, 1024], P(None, 'tile', None, 'depth')
- new_features: bfloat16 [16, 8192, 128], P('depth', 'tile')
- new_logits: float32 [16, 8192], P('depth', 'tile')
- shape_grads: float32 [2, 16, 5, 8192], P(None, 'depth', None, 'tile')
Inputs may be any that keep to these rules, and one draw needn't show every extreme that they name: `dest_slot`: for each view and layer no two splats share a slot; -1 marks a splat outside the view; a splat's place within its tile is its front-to-back order. At most 8 splats of one layer held by one index of tile go to the tiles of one index of tile, and in every view and layer there is an index of tile whose tiles receive exactly 8 from every owner, so that all their slots are used. `geometry`: components 0 and 1 are a splat's centre in pixels within its tile, from 0 to 32; components 2 and 3 lie in -0.5 to 2.0; component 4 in -0.6 to 0.6.
All inputs are finite; a program needn't handle non-finite values.
Results may differ from a plain program's by a relative error of at most 0.0073.
Values may be sent and summed in bfloat16 or wider, within the bound.
No kernel may reach another device: no remote copies, remote signals or barrier semaphores. Data moves between devices by JAX's collectives and lax.ppermute only.
A program may use at most 64 MiB of HBM per device.

v0:
```python
from functools import partial
import jax
import jax.numpy as jnp
from jax import lax
from jax.sharding import PartitionSpec as P

F = 128
W = 32
S = 128
VIEWS = 2
P_SIZE = 1024
clamp_top = 0.99
feature_rate = 0.5
opacity_rate = 0.5


def split_up(shard, dim, size):
    shape = shard.shape
    tiles = shard.reshape(*shape[:dim], size, shape[dim] // size, *shape[dim + 1 :])
    return jnp.moveaxis(tiles, dim, 0)


def sent_and_summed(shard, axis, dim):
    tiles = split_up(shard, dim, lax.axis_size(axis))
    arrived = lax.all_to_all(tiles, axis, split_axis=0, concat_axis=0, tiled=True)
    return arrived.astype(jnp.float32).sum(axis=0)


def joined_along(tiles, dim):
    tiles = jnp.moveaxis(tiles, 0, dim)
    shape = tiles.shape
    return tiles.reshape(*shape[:dim], shape[dim] * shape[dim + 1], *shape[dim + 2 :])


def from_everyone(shard, axis):
    copies = jnp.broadcast_to(shard, (lax.axis_size(axis), *shard.shape))
    return lax.all_to_all(copies, axis, split_axis=0, concat_axis=0, tiled=True)


def gather_directly(shard, axis, dim):
    return joined_along(from_everyone(shard, axis), dim)


def pixel_places():
    places = jnp.arange(P_SIZE, dtype=jnp.int32)
    across = (places % W).astype(jnp.float32) + 0.5
    downward = (places // W).astype(jnp.float32) + 0.5
    return (across, downward)


def block_sum(values, reverse):
    length = values.shape[0]
    block_rows = min(128, length)
    blocks = values.reshape(length // block_rows, block_rows, values.shape[1])
    positions = jnp.arange(block_rows)
    if reverse:
        triangle = (positions[:, None] < positions[None, :]).astype(jnp.float32)
    else:
        triangle = (positions[:, None] > positions[None, :]).astype(jnp.float32)
    within = jnp.einsum("ij,bjp->bip", triangle, blocks, precision=lax.Precision.HIGHEST)
    block_totals = jnp.sum(blocks, axis=1)
    if reverse:
        offsets = jnp.sum(block_totals, axis=0)[None, :] - jnp.cumsum(block_totals, axis=0)
    else:
        offsets = jnp.cumsum(block_totals, axis=0) - block_totals
    return (within + offsets[:, None, :]).reshape(length, values.shape[1])


def splat_fields(shapes):
    across, downward = pixel_places()
    delta_x = across[None, :] - shapes[0][:, None]
    delta_y = downward[None, :] - shapes[1][:, None]
    coef_a = jnp.exp(shapes[2])[:, None]
    coef_c = jnp.exp(shapes[3])[:, None]
    spread = jnp.exp(0.5 * (shapes[2] + shapes[3]))[:, None]
    coef_b = shapes[4][:, None] * spread
    quadric = (
        coef_a * delta_x * delta_x + 2.0 * coef_b * delta_x * delta_y + coef_c * delta_y * delta_y
    )
    falloff = jnp.exp(-0.5 * quadric)
    opacity = shapes[5][:, None]
    product = opacity * falloff
    coverage = jnp.minimum(product, clamp_top)
    return (delta_x, delta_y, coef_a, coef_b, coef_c, spread, falloff, opacity, product, coverage)


def layer_forward(inputs):
    slot_feats, shapes = inputs
    coverage = splat_fields(shapes)[9]
    log_keep = jnp.log(1.0 - coverage)
    before = block_sum(log_keep, False)
    weights = (coverage * jnp.exp(before)).astype(jnp.bfloat16)
    composite = lax.dot_general(
        slot_feats, weights, (((0,), (0,)), ((), ())), preferred_element_type=jnp.float32
    )
    layer_keep = jnp.exp(jnp.sum(log_keep, axis=0))
    return (composite, layer_keep)


def layer_backward(inputs):
    slot_feats, shapes, grad_comp, grad_keep = inputs
    delta_x, delta_y, coef_a, coef_b, coef_c, spread, falloff, opacity, product, coverage = (
        splat_fields(shapes)
    )
    log_keep = jnp.log(1.0 - coverage)
    before = block_sum(log_keep, False)
    decayed = jnp.exp(before)
    exact_weight = coverage * decayed
    weights = exact_weight.astype(jnp.bfloat16)
    layer_keep = jnp.exp(jnp.sum(log_keep, axis=0))
    grad_feat = lax.dot_general(
        weights, grad_comp, (((1,), (1,)), ((), ())), preferred_element_type=jnp.float32
    )
    grad_weight = jnp.dot(slot_feats, grad_comp, preferred_element_type=jnp.float32)
    grad_before = grad_weight * exact_weight
    later = block_sum(grad_before, True)
    grad_log = later + (grad_keep * layer_keep)[None, :]
    grad_coverage = grad_weight * decayed - grad_log / (1.0 - coverage)
    grad_product = jnp.where(product < clamp_top, grad_coverage, 0.0)
    grad_quadric = -0.5 * opacity * falloff * grad_product
    grad_mean_x = -2.0 * jnp.sum(grad_quadric * (coef_a * delta_x + coef_b * delta_y), axis=1)
    grad_mean_y = -2.0 * jnp.sum(grad_quadric * (coef_b * delta_x + coef_c * delta_y), axis=1)
    grad_first = jnp.sum(grad_quadric * delta_x * delta_x, axis=1)
    grad_cross = jnp.sum(grad_quadric * 2.0 * delta_x * delta_y, axis=1)
    grad_second = jnp.sum(grad_quadric * delta_y * delta_y, axis=1)
    grad_log_a = coef_a[:, 0] * grad_first + 0.5 * coef_b[:, 0] * grad_cross
    grad_log_c = coef_c[:, 0] * grad_second + 0.5 * coef_b[:, 0] * grad_cross
    grad_corr = spread[:, 0] * grad_cross
    opacity_flat = opacity[:, 0]
    grad_logit = opacity_flat * (1.0 - opacity_flat) * jnp.sum(falloff * grad_product, axis=1)
    grad_shape = jnp.stack(
        [grad_mean_x, grad_mean_y, grad_log_a, grad_log_c, grad_corr, grad_logit]
    )
    return (grad_feat, grad_shape)


def rear_step(all_keeps, all_terms, depth_here, layers, counter, carried):
    layer_at = layers - 1 - counter
    updated = all_terms[layer_at] + all_keeps[layer_at] * carried
    return jnp.where(layer_at > depth_here, updated, carried)


def body(features, logits, geometry, dest_slot, target):
    owners = lax.axis_size("tile")
    layers = lax.axis_size("depth")
    depth_here = lax.axis_index("depth")
    tiles_here = target.shape[1]
    owned = features.shape[1]
    capacity = owned // owners
    pixel_share = P_SIZE // layers
    splat_feats = features[0]
    logit_now = logits[0]
    images = []
    shape_grads = []
    for view_index in range(VIEWS):
        slot_ids = dest_slot[view_index, 0]
        visible = slot_ids >= 0
        receiver = jnp.where(visible, slot_ids // owned, owners)
        matches = (receiver[:, None] == jnp.arange(owners, dtype=jnp.int32)[None, :]).astype(
            jnp.int32
        )
        place_in = jnp.sum((jnp.cumsum(matches, axis=0) - matches) * matches, axis=1)
        position = jnp.where(visible, receiver * capacity + place_in, owners * capacity)
        local_slot = jnp.where(visible, slot_ids - receiver * owned, -1)
        opacity = jax.nn.sigmoid(logit_now)
        shape_rows = jnp.concatenate([geometry[view_index, 0], opacity[None, :]], axis=0).T
        row_buffer = (
            jnp.zeros((owners * capacity + 1, F), jnp.bfloat16)
            .at[position]
            .set(splat_feats)[:-1]
            .reshape(owners, capacity, F)
        )
        slot_buffer = (
            jnp.full((owners * capacity + 1,), -1, jnp.int32)
            .at[position]
            .set(local_slot)[:-1]
            .reshape(owners, capacity)
        )
        shape_buffer = (
            jnp.zeros((owners * capacity + 1, 6), jnp.float32)
            .at[position]
            .set(shape_rows)[:-1]
            .reshape(owners, capacity, 6)
        )
        got_rows, got_slots = (
            lax.all_to_all(row_buffer, "tile", split_axis=0, concat_axis=0, tiled=True),
            lax.all_to_all(slot_buffer, "tile", split_axis=0, concat_axis=0, tiled=True),
        )
        got_shapes = lax.all_to_all(shape_buffer, "tile", split_axis=0, concat_axis=0, tiled=True)
        arrived = got_slots.reshape(-1)
        present = arrived >= 0
        landing = jnp.where(present, arrived, owned)
        slot_feats = (
            jnp.zeros((owned + 1, F), jnp.bfloat16)
            .at[landing]
            .set(got_rows.reshape(-1, F))[:-1]
            .reshape(tiles_here, S, F)
        )
        slot_shapes = (
            jnp.zeros((owned + 1, 6), jnp.float32)
            .at[landing]
            .set(got_shapes.reshape(-1, 6))[:-1]
            .reshape(tiles_here, S, 6)
            .transpose(0, 2, 1)
        )
        composites, layer_keeps = lax.map(layer_forward, (slot_feats, slot_shapes))
        all_keeps = lax.all_gather(layer_keeps[None], "depth", axis=0, tiled=True)
        earlier_mask = (jnp.arange(layers) < depth_here)[:, None, None]
        ahead = jnp.prod(jnp.where(earlier_mask, all_keeps, 1.0), axis=0)
        contrib = ahead[:, None, :] * composites
        image_part = sent_and_summed(contrib.astype(jnp.bfloat16), "depth", 2)
        target_part = lax.dynamic_slice_in_dim(
            target[view_index], depth_here * pixel_share, pixel_share, 2
        ).astype(jnp.float32)
        residual = gather_directly(image_part - target_part, "depth", 2)
        images.append(image_part.astype(jnp.bfloat16))
        pixel_terms = jnp.sum(residual * composites, axis=1)
        all_terms = gather_directly(pixel_terms[None], "depth", 0)
        behind = lax.fori_loop(
            0,
            layers,
            partial(rear_step, all_keeps, all_terms, depth_here, layers),
            jnp.zeros_like(pixel_terms),
        )
        grad_keep = ahead * behind
        grad_comp = (ahead[:, None, :] * residual).astype(jnp.bfloat16)
        grad_feat, grad_shape = lax.map(
            layer_backward, (slot_feats, slot_shapes, grad_comp, grad_keep)
        )
        flat_feat = grad_feat.reshape(owned, F)
        flat_shape = grad_shape.transpose(0, 2, 1).reshape(owned, 6)
        fetched = jnp.where(present, arrived, 0)
        back_feat = jnp.where(present[:, None], flat_feat[fetched], 0.0).reshape(
            owners, capacity, F
        )
        back_shape = jnp.where(present[:, None], flat_shape[fetched], 0.0).reshape(
            owners, capacity, 6
        )
        return_feat, return_shape = (
            lax.all_to_all(back_feat, "tile", split_axis=0, concat_axis=0, tiled=True),
            lax.all_to_all(back_shape, "tile", split_axis=0, concat_axis=0, tiled=True),
        )
        padded_feat = jnp.concatenate(
            [return_feat.reshape(-1, F), jnp.zeros((1, F), jnp.float32)], axis=0
        )
        padded_shape = jnp.concatenate(
            [return_shape.reshape(-1, 6), jnp.zeros((1, 6), jnp.float32)], axis=0
        )
        splat_grad_feat = padded_feat[position]
        splat_grad_shape = padded_shape[position]
        shape_grads.append(splat_grad_shape[:, :5].T)
        splat_feats = (splat_feats.astype(jnp.float32) - feature_rate * splat_grad_feat).astype(
            jnp.bfloat16
        )
        logit_now = logit_now - opacity_rate * splat_grad_shape[:, 5]
    return (jnp.stack(images), splat_feats[None], logit_now[None], jnp.stack(shape_grads)[:, None])


def solution(mesh):
    placed = (
        P("depth", "tile", None),
        P("depth", "tile"),
        P(None, "depth", None, "tile"),
        P(None, "depth", "tile"),
        P(None, "tile", None, None),
    )
    return jax.shard_map(
        body,
        mesh=mesh,
        in_specs=placed,
        out_specs=(
            P(None, "tile", None, "depth"),
            P("depth", "tile", None),
            P("depth", "tile"),
            P(None, "depth", None, "tile"),
        ),
        check_vma=False,
    )
```

profile of v0, /device:TPU:1, one launch (start us, length us, event | category | flops | bytes accessed | tf_op | source)
XLA Modules:
  0.0 448.0 jit_solution(14896957817625969627)
XLA Ops:
  6.5 1.4 scatter_custom_fusion
  8.6 10.4 %all-to-all-start = ((s32[32,1,8]{2,1,0:T(1,128)}), s32[32,1,8]{2,1,0:T(1,128)S(1)}, u32[]{:S(2)}, u32[]{:S(2)}) async-start(s32[32,1,8]{2,1,0:T(1,128)} %bitcast.92), calls=%async_computation | async-start | bytes 32768 | tf_op jit(solution)/shard_map/all_to_all | solution.py:187
  23.8 2.3 all-to-all-done
  26.1 5.2 %all-to-all-start.2 = ((f32[32,8,6]{2,1,0:T(8,128)}), f32[32,8,6]{2,1,0:T(8,128)S(1)}, u32[]{:S(2)}, u32[]{:S(2)}) async-start(f32[32,8,6]{2,1,0:T(8,128)} %slice_bitcast_fusion.15), calls=%async_computation.2 | async-start | bytes 262144 | tf_op jit(solution)/shard_map/all_to_all | solution.py:189
  32.6 6.3 %all-to-all-done.2 = f32[32,8,6]{2,1,0:T(8,128)S(1)} async-done(((f32[32,8,6]{2,1,0:T(8,128)}), f32[32,8,6]{2,1,0:T(8,128)S(1)}, u32[]{:S(2)}, u32[]{:S(2)}) %all-to-all-start.2) | async-done | bytes 6176 | tf_op jit(solution)/shard_map/all_to_all | solution.py:189
  38.9 3.9 all-to-all-start.1
  44.1 6.2 %all-to-all-done.1 = bf16[32,8,128]{2,1,0:T(8,128)(2,1)S(1)} async-done(((bf16[32,8,128]{2,1,0:T(8,128)(2,1)}), bf16[32,8,128]{2,1,0:T(8,128)(2,1)S(1)}, u32[]{:S(2)}, u32[]{:S(2)}) %all-to-all-start.1) | async-done | bytes 65568 | tf_op jit(solution)/shard_map/all_to_all | solution.py:186
  52.9 5.0 %while.88 = (s32[]{:T(128)}, f32[2,128,1024]{1,2,0:T(8,128)S(1)}, f32[2,1024]{1,0:T(2,128)S(1)}, bf16[2,128,128]{2,1,0:T(8,128)(2,1)S(1)}, f32[2,6,128]{2,1,0:T(8,128)S(1)}, /*index=5*/s32[]{:T(128)}, s32[]{:T(128)}) while((s32[]{:T(128)}, f32[2,128,1024]{1,2,0:T(8,128)S(1)}, f32[2,1024]{1,0:T(2,128)S(1)}, ...), condition=%wide.region_11.12_spmd, body=%wide.region_8.11_spmd.sunk | while | flops 242777600 | bytes 1177685 | solution.py:206
  53.4 1.2 fusion.322
  55.9 1.2 fusion.322
  57.9 27.0 %all-gather.2 = f32[16,2,1024]{2,1,0:T(2,128)S(1)} all-gather(f32[1,2,1024]{2,1,0:T(2,128)S(1)} %bitcast.719), channel_id=2, replica_groups=mesh['tile'=32,'depth'=16] {'depth'}, dimensions={0}, use_global_device_ids=true | all-gather | bytes 139264 | tf_op jit(solution)/shard_map/all_gather | solution.py:207
  86.2 6.7 %all-to-all-start.3 = ((bf16[16,2,128,64]{2,3,1,0:T(8,128)(2,1)}), bf16[16,2,128,64]{2,3,1,0:T(8,128)(2,1)S(1)}, u32[]{:S(2)}, u32[]{:S(2)}) async-start(bf16[16,2,128,64]{2,3,1,0:T(8,128)(2,1)} %copy.118), calls=%async_computation.3 | async-start | bytes 1048576 | tf_op jit(solution)/shard_map/all_to_all | solution.py:25
  93.2 18.2 %all-to-all-done.3 = bf16[16,2,128,64]{2,3,1,0:T(8,128)(2,1)S(1)} async-done(((bf16[16,2,128,64]{2,3,1,0:T(8,128)(2,1)}), bf16[16,2,128,64]{2,3,1,0:T(8,128)(2,1)S(1)}, u32[]{:S(2)}, u32[]{:S(2)}) %all-to-all-start.3) | async-done | bytes 524320 | tf_op jit(solution)/shard_map/all_to_all | solution.py:25
  112.7 13.6 %all-to-all-start.5 = ((f32[16,2,128,64]{2,3,1,0:T(8,128)}), f32[16,2,128,64]{2,3,1,0:T(8,128)S(1)}, u32[]{:S(2)}, u32[]{:S(2)}) async-start(f32[16,2,128,64]{2,3,1,0:T(8,128)} %broadcast_in_dim.232), calls=%async_computation.5 | async-start | bytes 2097152 | tf_op jit(solution)/shard_map/all_to_all | solution.py:37
  126.3 1.4 scatter_custom_fusion.5
  128.4 42.7 %all-to-all-done.5 = f32[16,2,128,64]{2,3,1,0:T(8,128)S(1)} async-done(((f32[16,2,128,64]{2,3,1,0:T(8,128)}), f32[16,2,128,64]{2,3,1,0:T(8,128)S(1)}, u32[]{:S(2)}, u32[]{:S(2)}) %all-to-all-start.5) | async-done | bytes 1048608 | tf_op jit(solution)/shard_map/all_to_all | solution.py:37
  171.1 8.5 %all-to-all-start.4 = ((s32[32,1,8]{2,1,0:T(1,128)}), s32[32,1,8]{2,1,0:T(1,128)S(1)}, u32[]{:S(2)}, u32[]{:S(2)}) async-start(s32[32,1,8]{2,1,0:T(1,128)} %bitcast.113), calls=%async_computation.4 | async-start | bytes 32768 | tf_op jit(solution)/shard_map/all_to_all | solution.py:187
  180.4 6.2 %all-to-all-done.4 = s32[32,1,8]{2,1,0:T(1,128)S(1)} async-done(((s32[32,1,8]{2,1,0:T(1,128)}), s32[32,1,8]{2,1,0:T(1,128)S(1)}, u32[]{:S(2)}, u32[]{:S(2)}) %all-to-all-start.4) | async-done | bytes 1056 | tf_op jit(solution)/shard_map/all_to_all | solution.py:187
  187.3 8.8 %all-to-all-start.6 = ((f32[16,1,2,1024]{3,2,1,0:T(2,128)}), f32[16,1,2,1024]{3,2,1,0:T(2,128)S(1)}, u32[]{:S(2)}, u32[]{:S(2)}) async-start(f32[16,1,2,1024]{3,2,1,0:T(2,128)} %broadcast_in_dim.233), calls=%async_computation.6 | async-start | bytes 262144 | tf_op jit(solution)/shard_map/all_to_all | solution.py:37
  197.1 11.0 %all-to-all-done.6 = f32[16,1,2,1024]{3,2,1,0:T(2,128)S(1)} async-done(((f32[16,1,2,1024]{3,2,1,0:T(2,128)}), f32[16,1,2,1024]{3,2,1,0:T(2,128)S(1)}, u32[]{:S(2)}, u32[]{:S(2)}) %all-to-all-start.6) | async-done | bytes 131104 | tf_op jit(solution)/shard_map/all_to_all | solution.py:37
  209.0 9.3 %while.89 = (s32[]{:T(128)}, f32[2,128,128]{2,1,0:T(8,128)S(1)}, f32[2,6,128]{2,1,0:T(8,128)S(1)}, f32[2,6,128]{2,1,0:T(8,128)S(1)}, bf16[2,128,1024]{1,2,0:T(8,...) while((s32[]{:T(128)}, f32[2,128,128]{2,1,0:T(8,128)S(1)}, ...), condition=%wide.region_31.32_spmd, body=%wide.region_21.31_spmd.sunk | while | flops 485672448 | bytes 3947105 | solution.py:227
  211.0 1.9 fusion.332
  215.7 1.9 fusion.332
  219.9 7.2 %all-to-all-start.9 = ((f32[32,8,6]{2,1,0:T(8,128)}), f32[32,8,6]{2,1,0:T(8,128)S(1)}, u32[]{:S(2)}, u32[]{:S(2)}) async-start(f32[32,8,6]{2,1,0:T(8,128)} %bitcast_select_fusion.2), calls=%async_computation.9 | async-start | bytes 262144 | tf_op jit(solution)/shard_map/all_to_all | solution.py:241
  228.6 6.2 %all-to-all-done.9 = f32[32,8,6]{2,1,0:T(8,128)S(1)} async-done(((f32[32,8,6]{2,1,0:T(8,128)}), f32[32,8,6]{2,1,0:T(8,128)S(1)}, u32[]{:S(2)}, u32[]{:S(2)}) %all-to-all-start.9) | async-done | bytes 6176 | tf_op jit(solution)/shard_map/all_to_all | solution.py:241
  234.8 3.9 all-to-all-start.7
  241.7 4.8 %all-to-all-done.7 = f32[32,8,128]{2,1,0:T(8,128)S(1)} async-done(((f32[32,8,128]{2,1,0:T(8,128)}), f32[32,8,128]{2,1,0:T(8,128)S(1)}, u32[]{:S(2)}, u32[]{:S(2)}) %all-to-all-start.7) | async-done | bytes 131104 | tf_op jit(solution)/shard_map/all_to_all | solution.py:240
  246.5 3.9 all-to-all-start.10
  253.0 5.1 %all-to-all-done.10 = f32[32,8,6]{2,1,0:T(8,128)S(1)} async-done(((f32[32,8,6]{2,1,0:T(8,128)}), f32[32,8,6]{2,1,0:T(8,128)S(1)}, u32[]{:S(2)}, u32[]{:S(2)}) %all-to-all-start.10) | async-done | bytes 6176 | tf_op jit(solution)/shard_map/all_to_all | solution.py:189
  258.1 3.9 all-to-all-start.8
  263.3 6.2 %all-to-all-done.8 = bf16[32,8,128]{2,1,0:T(8,128)(2,1)S(1)} async-done(((bf16[32,8,128]{2,1,0:T(8,128)(2,1)}), bf16[32,8,128]{2,1,0:T(8,128)(2,1)S(1)}, u32[]{:S(2)}, u32[]{:S(2)}) %all-to-all-start.8) | async-done | bytes 65568 | tf_op jit(solution)/shard_map/all_to_all | solution.py:186
  272.1 5.0 %while.90 = (s32[]{:T(128)}, f32[2,128,1024]{1,2,0:T(8,128)S(1)}, f32[2,1024]{1,0:T(2,128)S(1)}, bf16[2,128,128]{2,1,0:T(8,128)(2,1)S(1)}, f32[2,6,128]{2,1,0:T(8,128)S(1)}, /*index=5*/s32[]{:T(128)}, s32[]{:T(128)}) while((s32[]{:T(128)}, f32[2,128,1024]{1,2,0:T(8,128)S(1)}, f32[2,1024]{1,0:T(2,128)S(1)}, ...), condition=%wide.region_39.40_spmd, body=%wide.region_36.39_spmd.sunk | while | flops 242777600 | bytes 1177685 | solution.py:206
  272.6 1.2 fusion.338
  275.2 1.2 fusion.338
  277.1 21.9 %all-gather.3 = f32[16,2,1024]{2,1,0:T(2,128)S(1)} all-gather(f32[1,2,1024]{2,1,0:T(2,128)S(1)} %bitcast.721), channel_id=3, replica_groups=mesh['tile'=32,'depth'=16] {'depth'}, dimensions={0}, use_global_device_ids=true | all-gather | bytes 139264 | tf_op jit(solution)/shard_map/all_gather | solution.py:207
  300.3 4.1 all-to-all-start.11
  304.6 18.2 %all-to-all-done.11 = bf16[16,2,128,64]{2,3,1,0:T(8,128)(2,1)S(1)} async-done(((bf16[16,2,128,64]{2,3,1,0:T(8,128)(2,1)}), bf16[16,2,128,64]{2,3,1,0:T(8,128)(2,1)S(1)}, u32[]{:S(2)}, u32[]{:S(2)}) %all-to-all-start.11) | async-done | bytes 524320 | tf_op jit(solution)/shard_map/all_to_all | solution.py:25
  324.0 13.6 %all-to-all-start.12 = ((f32[16,2,128,64]{2,3,1,0:T(8,128)}), f32[16,2,128,64]{2,3,1,0:T(8,128)S(1)}, u32[]{:S(2)}, u32[]{:S(2)}) async-start(f32[16,2,128,64]{2,3,1,0:T(8,128)} %broadcast_in_dim.239), calls=%async_computation.12 | async-start | bytes 2097152 | tf_op jit(solution)/shard_map/all_to_all | solution.py:37
  337.7 44.8 %all-to-all-done.12 = f32[16,2,128,64]{2,3,1,0:T(8,128)S(1)} async-done(((f32[16,2,128,64]{2,3,1,0:T(8,128)}), f32[16,2,128,64]{2,3,1,0:T(8,128)S(1)}, u32[]{:S(2)}, u32[]{:S(2)}) %all-to-all-start.12) | async-done | bytes 1048608 | tf_op jit(solution)/shard_map/all_to_all | solution.py:37
  383.9 12.4 %all-to-all-start.13 = ((f32[16,1,2,1024]{3,2,1,0:T(2,128)}), f32[16,1,2,1024]{3,2,1,0:T(2,128)S(1)}, u32[]{:S(2)}, u32[]{:S(2)}) async-start(f32[16,1,2,1024]{3,2,1,0:T(2,128)} %broadcast_in_dim.240), calls=%async_computation.13 | async-start | bytes 262144 | tf_op jit(solution)/shard_map/all_to_all | solution.py:37
  397.2 11.1 %all-to-all-done.13 = f32[16,1,2,1024]{3,2,1,0:T(2,128)S(1)} async-done(((f32[16,1,2,1024]{3,2,1,0:T(2,128)}), f32[16,1,2,1024]{3,2,1,0:T(2,128)S(1)}, u32[]{:S(2)}, u32[]{:S(2)}) %all-to-all-start.13) | async-done | bytes 131104 | tf_op jit(solution)/shard_map/all_to_all | solution.py:37
  409.2 9.1 %while.91 = (s32[]{:T(128)}, f32[2,128,128]{2,1,0:T(8,128)S(1)}, f32[2,6,128]{2,1,0:T(8,128)S(1)}, f32[2,6,128]{2,1,0:T(8,128)S(1)}, bf16[2,128,1024]{1,2,0:T(8,...) while((s32[]{:T(128)}, f32[2,128,128]{2,1,0:T(8,128)S(1)}, ...), condition=%wide.region_55.56_spmd, body=%wide.region_45.55_spmd.sunk | while | flops 485672448 | bytes 3947105 | solution.py:227
  411.2 1.9 fusion.348
  415.8 1.9 fusion.348
  419.9 7.3 %all-to-all-start.15 = ((f32[32,8,6]{2,1,0:T(8,128)}), f32[32,8,6]{2,1,0:T(8,128)S(1)}, u32[]{:S(2)}, u32[]{:S(2)}) async-start(f32[32,8,6]{2,1,0:T(8,128)} %bitcast_select_fusion), calls=%async_computation.15 | async-start | bytes 262144 | tf_op jit(solution)/shard_map/all_to_all | solution.py:241
  428.7 6.2 %all-to-all-done.15 = f32[32,8,6]{2,1,0:T(8,128)S(1)} async-done(((f32[32,8,6]{2,1,0:T(8,128)}), f32[32,8,6]{2,1,0:T(8,128)S(1)}, u32[]{:S(2)}, u32[]{:S(2)}) %all-to-all-start.15) | async-done | bytes 6176 | tf_op jit(solution)/shard_map/all_to_all | solution.py:241
  434.9 3.9 all-to-all-start.14
  441.1 5.5 %all-to-all-done.14 = f32[32,8,128]{2,1,0:T(8,128)S(1)} async-done(((f32[32,8,128]{2,1,0:T(8,128)}), f32[32,8,128]{2,1,0:T(8,128)S(1)}, u32[]{:S(2)}, u32[]{:S(2)}) %all-to-all-start.14) | async-done | bytes 131104 | tf_op jit(solution)/shard_map/all_to_all | solution.py:240
  (290 shorter events, 63.8 us)
Async XLA Ops:
  2.2 0.6 copy-start.6
  3.6 0.6 copy-start.7
  4.2 0.7 slice-start.2
  5.0 0.7 slice-start.3
  5.8 0.7 copy-start.5
  8.6 10.5 %copy-start.4 = (f32[2,1,5,256]{3,1,2,0:T(1,128)S(1)}, f32[2,1,5,256]{3,1,2,0:T(1,128)}, u32[]{:S(2)}) copy-start(f32[2,1,5,256]{3,1,2,0:T(1,128)} %param.19) | copy-start | bytes 30724
  8.6 17.5 %all-to-all-start = ((s32[32,1,8]{2,1,0:T(1,128)}), s32[32,1,8]{2,1,0:T(1,128)S(1)}, u32[]{:S(2)}, u32[]{:S(2)}) async-start(s32[32,1,8]{2,1,0:T(1,128)} %bitcast.92), calls=%async_computation | async-start | bytes 32768 | tf_op jit(solution)/shard_map/all_to_all | solution.py:187
  19.1 0.7 copy-start.8
  21.1 0.8 copy-start.3
  26.1 12.8 %all-to-all-start.2 = ((f32[32,8,6]{2,1,0:T(8,128)}), f32[32,8,6]{2,1,0:T(8,128)S(1)}, u32[]{:S(2)}, u32[]{:S(2)}) async-start(f32[32,8,6]{2,1,0:T(8,128)} %slice_bitcast_fusion.15), calls=%async_computation.2 | async-start | bytes 262144 | tf_op jit(solution)/shard_map/all_to_all | solution.py:189
  38.9 11.4 %all-to-all-start.1 = ((bf16[32,8,128]{2,1,0:T(8,128)(2,1)}), bf16[32,8,128]{2,1,0:T(8,128)(2,1)S(1)}, u32[]{:S(2)}, u32[]{:S(2)}) async-start(bf16[32,8,128]{2,1,0:T(8,128)(2,1)} %slice_bitcast_fusion.17), calls=%async_computation.1 | async-start | bytes 131072 | tf_op jit(solution)/shard_map/all_to_all | solution.py:186
  51.4 0.6 copy-start.1
  52.0 0.8 slice-start
  85.4 7.6 %copy-start = (bf16[2,2,128,1024]{3,2,1,0:T(8,128)(2,1)S(1)}, bf16[2,2,128,1024]{3,2,1,0:T(8,128)(2,1)}, u32[]{:S(2)}) copy-start(bf16[2,2,128,1024]{3,2,1,0:T(8,128)(2,1)} %param.21) | copy-start | bytes 3145732
  86.2 25.2 %all-to-all-start.3 = ((bf16[16,2,128,64]{2,3,1,0:T(8,128)(2,1)}), bf16[16,2,128,64]{2,3,1,0:T(8,128)(2,1)S(1)}, u32[]{:S(2)}, u32[]{:S(2)}) async-start(bf16[16,2,128,64]{2,3,1,0:T(8,128)(2,1)} %copy.118), calls=%async_computation.3 | async-start | bytes 1048576 | tf_op jit(solution)/shard_map/all_to_all | solution.py:25
  112.7 58.4 %all-to-all-start.5 = ((f32[16,2,128,64]{2,3,1,0:T(8,128)}), f32[16,2,128,64]{2,3,1,0:T(8,128)S(1)}, u32[]{:S(2)}, u32[]{:S(2)}) async-start(f32[16,2,128,64]{2,3,1,0:T(8,128)} %broadcast_in_dim.232), calls=%async_computation.5 | async-start | bytes 2097152 | tf_op jit(solution)/shard_map/all_to_all | solution.py:37
  171.1 15.5 %all-to-all-start.4 = ((s32[32,1,8]{2,1,0:T(1,128)}), s32[32,1,8]{2,1,0:T(1,128)S(1)}, u32[]{:S(2)}, u32[]{:S(2)}) async-start(s32[32,1,8]{2,1,0:T(1,128)} %bitcast.113), calls=%async_computation.4 | async-start | bytes 32768 | tf_op jit(solution)/shard_map/all_to_all | solution.py:187
  187.3 20.8 %all-to-all-start.6 = ((f32[16,1,2,1024]{3,2,1,0:T(2,128)}), f32[16,1,2,1024]{3,2,1,0:T(2,128)S(1)}, u32[]{:S(2)}, u32[]{:S(2)}) async-start(f32[16,1,2,1024]{3,2,1,0:T(2,128)} %broadcast_in_dim.233), calls=%async_computation.6 | async-start | bytes 262144 | tf_op jit(solution)/shard_map/all_to_all | solution.py:37
  219.9 15.0 %all-to-all-start.9 = ((f32[32,8,6]{2,1,0:T(8,128)}), f32[32,8,6]{2,1,0:T(8,128)S(1)}, u32[]{:S(2)}, u32[]{:S(2)}) async-start(f32[32,8,6]{2,1,0:T(8,128)} %bitcast_select_fusion.2), calls=%async_computation.9 | async-start | bytes 262144 | tf_op jit(solution)/shard_map/all_to_all | solution.py:241
  234.8 11.6 %all-to-all-start.7 = ((f32[32,8,128]{2,1,0:T(8,128)}), f32[32,8,128]{2,1,0:T(8,128)S(1)}, u32[]{:S(2)}, u32[]{:S(2)}) async-start(f32[32,8,128]{2,1,0:T(8,128)} %bitcast_select_fusion.3), calls=%async_computation.7 | async-start | bytes 262144 | tf_op jit(solution)/shard_map/all_to_all | solution.py:240
  246.5 11.6 %all-to-all-start.10 = ((f32[32,8,6]{2,1,0:T(8,128)}), f32[32,8,6]{2,1,0:T(8,128)S(1)}, u32[]{:S(2)}, u32[]{:S(2)}) async-start(f32[32,8,6]{2,1,0:T(8,128)} %slice_bitcast_fusion.14), calls=%async_computation.10 | async-start | bytes 262144 | tf_op jit(solution)/shard_map/all_to_all | solution.py:189
  258.1 11.4 %all-to-all-start.8 = ((bf16[32,8,128]{2,1,0:T(8,128)(2,1)}), bf16[32,8,128]{2,1,0:T(8,128)(2,1)S(1)}, u32[]{:S(2)}, u32[]{:S(2)}) async-start(bf16[32,8,128]{2,1,0:T(8,128)(2,1)} %slice_bitcast_fusion.16), calls=%async_computation.8 | async-start | bytes 131072 | tf_op jit(solution)/shard_map/all_to_all | solution.py:186
  270.6 0.6 copy-start.2
  271.3 0.8 slice-start.1
  300.3 22.5 %all-to-all-start.11 = ((bf16[16,2,128,64]{2,3,1,0:T(8,128)(2,1)}), bf16[16,2,128,64]{2,3,1,0:T(8,128)(2,1)S(1)}, u32[]{:S(2)}, u32[]{:S(2)}) async-start(bf16[16,2,128,64]{2,3,1,0:T(8,128)(2,1)} %copy.132), calls=%async_computation.11 | async-start | bytes 1048576 | tf_op jit(solution)/shard_map/all_to_all | solution.py:25
  324.0 58.5 %all-to-all-start.12 = ((f32[16,2,128,64]{2,3,1,0:T(8,128)}), f32[16,2,128,64]{2,3,1,0:T(8,128)S(1)}, u32[]{:S(2)}, u32[]{:S(2)}) async-start(f32[16,2,128,64]{2,3,1,0:T(8,128)} %broadcast_in_dim.239), calls=%async_computation.12 | async-start | bytes 2097152 | tf_op jit(solution)/shard_map/all_to_all | solution.py:37
  383.9 24.4 %all-to-all-start.13 = ((f32[16,1,2,1024]{3,2,1,0:T(2,128)}), f32[16,1,2,1024]{3,2,1,0:T(2,128)S(1)}, u32[]{:S(2)}, u32[]{:S(2)}) async-start(f32[16,1,2,1024]{3,2,1,0:T(2,128)} %broadcast_in_dim.240), calls=%async_computation.13 | async-start | bytes 262144 | tf_op jit(solution)/shard_map/all_to_all | solution.py:37
  419.9 15.0 %all-to-all-start.15 = ((f32[32,8,6]{2,1,0:T(8,128)}), f32[32,8,6]{2,1,0:T(8,128)S(1)}, u32[]{:S(2)}, u32[]{:S(2)}) async-start(f32[32,8,6]{2,1,0:T(8,128)} %bitcast_select_fusion), calls=%async_computation.15 | async-start | bytes 262144 | tf_op jit(solution)/shard_map/all_to_all | solution.py:241
  434.9 11.6 %all-to-all-start.14 = ((f32[32,8,128]{2,1,0:T(8,128)}), f32[32,8,128]{2,1,0:T(8,128)S(1)}, u32[]{:S(2)}, u32[]{:S(2)}) async-start(f32[32,8,128]{2,1,0:T(8,128)} %bitcast_select_fusion.1), calls=%async_computation.14 | async-start | bytes 262144 | tf_op jit(solution)/shard_map/all_to_all | solution.py:240
where the time goes:
time: 450 us; the launch traced here: 448 us
  waiting for transfers between devices  201 us (45%)
  starting transfers between devices  118 us (26%)
  blocking collectives  48.9 us (11%)
  local copies, waits for them, and re-layouts  37.7 us (8%)
  matrix products  21.2 us (5%)
  other arithmetic  18.5 us (4%)
    all_to_all x4, waiting for transfers between devices, from_everyone(): return lax.all_to_all(copies, axis, split_axis=0, concat_axis=0, tiled=True)  110 us
    all_gather x2, blocking collectives, body(): all_keeps = lax.all_gather(layer_keeps[None], 'depth', axis=0, tiled=True)  48.9 us
    all_to_all x4, starting transfers between devices, from_everyone(): return lax.all_to_all(copies, axis, split_axis=0, concat_axis=0, tiled=True)  48.4 us
    all_to_all x2, waiting for transfers between devices, sent_and_summed(): lax.all_to_all(tiles, axis, split_axis=0, concat_axis=0, tiled=True)  36.4 us
    all_to_all x2, starting transfers between devices, body(): lax.all_to_all(slot_buffer, 'tile', split_axis=0, concat_axis=0, tiled=True)  19 us
    dot_general x12, matrix products, block_sum(): jnp.einsum('ij,bjp->bip', triangle, blocks, precision=lax.Precision.HIGHEST)  15.4 us
    all_to_all x2, starting transfers between devices, body(): lax.all_to_all(back_shape, 'tile', split_axis=0, concat_axis=0, tiled=True)  14.5 us
    all_to_all x2, waiting for transfers between devices, body(): lax.all_to_all(back_shape, 'tile', split_axis=0, concat_axis=0, tiled=True)  12.5 us
  transfers between devices with their start and end apart: 16, of which 16 were waited for; matrix products, arithmetic and copies ran while one was open for 5% of the time, Pallas kernels for 0%

commit v1 on v0

--- a/solution.py
+++ b/solution.py
@@ -204,7 +204,9 @@
             .transpose(0, 2, 1)
         )
         composites, layer_keeps = lax.map(layer_forward, (slot_feats, slot_shapes))
-        all_keeps = lax.all_gather(layer_keeps[None], "depth", axis=0, tiled=True)
+        x = layer_keeps[None]
+        sent = jnp.stack([x] * lax.axis_size("depth"))
+        all_keeps = jnp.concatenate(lax.all_to_all(sent, "depth", 0, 0), axis=0)
         earlier_mask = (jnp.arange(layers) < depth_here)[:, None, None]
         ahead = jnp.prod(jnp.where(earlier_mask, all_keeps, 1.0), axis=0)
         contrib = ahead[:, None, :] * composites

time: 450 us -> 451 us (level)
  blocking collectives: 48.9 us -> 15.4 us
  waiting for transfers between devices: 201 us -> 223 us
  starting transfers between devices: 118 us -> 129 us
    all_gather x2 -> x0, blocking collectives: 48.9 us -> none  [body(): all_keeps = lax.all_gather(layer_keeps[None], 'depth', axis=0, tiled=True)]
    all_to_all x0 -> x1, blocking collectives: none -> 15.4 us  [body(): all_keeps = jnp.concatenate(lax.all_to_all(sent, 'depth', 0, 0), axis=0)]
    all_to_all x0 -> x1, starting transfers between devices: none -> 13.1 us  [body(): all_keeps = jnp.concatenate(lax.all_to_all(sent, 'depth', 0, 0), axis=0)]
    all_to_all x0 -> x1, waiting for transfers between devices: none -> 12.1 us  [body(): all_keeps = jnp.concatenate(lax.all_to_all(sent, 'depth', 0, 0), axis=0)]
    all_to_all x2, waiting for transfers between devices: 36.4 us -> 45.4 us  [sent_and_summed(): lax.all_to_all(tiles, axis, split_axis=0, concat_axis=0, tiled=True)]
  transfers between devices with their start and end apart: 16 -> 17, of which waited for: 16 -> 17; matrix products, arithmetic and copies ran while one was open for 5% -> 5% of each run, Pallas kernels for 0% -> 0%
where the time goes in v1:
time: 451 us; the launch traced here: 449 us
  waiting for transfers between devices  223 us (49%)
  starting transfers between devices  129 us (29%)
  local copies, waits for them, and re-layouts  38.7 us (9%)
  matrix products  21.2 us (5%)
  other arithmetic  18.5 us (4%)
  blocking collectives  15.4 us (3%)
    all_to_all x4, waiting for transfers between devices, from_everyone(): return lax.all_to_all(copies, axis, split_axis=0, concat_axis=0, tiled=True)  110 us
    all_to_all x4, starting transfers between devices, from_everyone(): return lax.all_to_all(copies, axis, split_axis=0, concat_axis=0, tiled=True)  45.5 us
    all_to_all x2, waiting for transfers between devices, sent_and_summed(): lax.all_to_all(tiles, axis, split_axis=0, concat_axis=0, tiled=True)  45.4 us
    all_to_all x2, starting transfers between devices, body(): lax.all_to_all(slot_buffer, 'tile', split_axis=0, concat_axis=0, tiled=True)  19.7 us
    dot_general x12, matrix products, block_sum(): jnp.einsum('ij,bjp->bip', triangle, blocks, precision=lax.Precision.HIGHEST)  15.4 us
    all_to_all x1, blocking collectives, body(): all_keeps = jnp.concatenate(lax.all_to_all(sent, 'depth', 0, 0), axis=0)  15.4 us
    all_to_all x2, starting transfers between devices, body(): lax.all_to_all(back_shape, 'tile', split_axis=0, concat_axis=0, tiled=True)  14.1 us
    all_to_all x1, starting transfers between devices, body(): all_keeps = jnp.concatenate(lax.all_to_all(sent, 'depth', 0, 0), axis=0)  13.1 us
  transfers between devices with their start and end apart: 17, of which 17 were waited for; matrix products, arithmetic and copies ran while one was open for 5% of the time, Pallas kernels for 0%

profile of v1, /device:TPU:1, one launch (start us, length us, event | category | flops | bytes accessed | tf_op | source)
XLA Modules:
  0.0 449.2 jit_solution(6436275001941145879)
XLA Ops:
  6.5 1.4 scatter_custom_fusion
  8.6 10.5 %all-to-all-start = ((s32[32,1,8]{2,1,0:T(1,128)}), s32[32,1,8]{2,1,0:T(1,128)S(1)}, u32[]{:S(2)}, u32[]{:S(2)}) async-start(s32[32,1,8]{2,1,0:T(1,128)} %bitcast.92), calls=%async_computation | async-start | bytes 32768 | tf_op jit(solution)/shard_map/all_to_all | solution.py:187
  23.1 2.9 all-to-all-done
  26.1 4.6 %all-to-all-start.2 = ((f32[32,8,6]{2,1,0:T(8,128)}), f32[32,8,6]{2,1,0:T(8,128)S(1)}, u32[]{:S(2)}, u32[]{:S(2)}) async-start(f32[32,8,6]{2,1,0:T(8,128)} %slice_bitcast_fusion.15), calls=%async_computation.2 | async-start | bytes 262144 | tf_op jit(solution)/shard_map/all_to_all | solution.py:189
  32.6 5.7 %all-to-all-done.2 = f32[32,8,6]{2,1,0:T(8,128)S(1)} async-done(((f32[32,8,6]{2,1,0:T(8,128)}), f32[32,8,6]{2,1,0:T(8,128)S(1)}, u32[]{:S(2)}, u32[]{:S(2)}) %all-to-all-start.2) | async-done | bytes 6176 | tf_op jit(solution)/shard_map/all_to_all | solution.py:189
  38.2 3.9 all-to-all-start.1
  43.4 6.2 %all-to-all-done.1 = bf16[32,8,128]{2,1,0:T(8,128)(2,1)S(1)} async-done(((bf16[32,8,128]{2,1,0:T(8,128)(2,1)}), bf16[32,8,128]{2,1,0:T(8,128)(2,1)S(1)}, u32[]{:S(2)}, u32[]{:S(2)}) %all-to-all-start.1) | async-done | bytes 65568 | tf_op jit(solution)/shard_map/all_to_all | solution.py:186
  52.3 5.0 %while.88 = (s32[]{:T(128)}, f32[2,128,1024]{1,2,0:T(8,128)S(1)}, f32[2,1024]{1,0:T(2,128)S(1)}, bf16[2,128,128]{2,1,0:T(8,128)(2,1)S(1)}, f32[2,6,128]{2,1,0:T(8,128)S(1)}, /*index=5*/s32[]{:T(128)}, s32[]{:T(128)}) while((s32[]{:T(128)}, f32[2,128,1024]{1,2,0:T(8,128)S(1)}, f32[2,1024]{1,0:T(2,128)S(1)}, ...), condition=%wide.region_11.12_spmd, body=%wide.region_8.11_spmd.sunk | while | flops 242777600 | bytes 1177685 | solution.py:206
  52.8 1.2 fusion.322
  57.9 13.1 %all-to-all-start.3 = ((f32[16,1,2,1024]{3,2,1,0:T(2,128)}), f32[16,1,2,1024]{3,2,1,0:T(2,128)S(1)}, u32[]{:S(2)}, u32[]{:S(2)}) async-start(f32[16,1,2,1024]{3,2,1,0:T(2,128)} %stack.44), calls=%async_computation.3 | async-start | bytes 262144 | tf_op jit(solution)/shard_map/all_to_all | solution.py:209
  71.0 12.1 %all-to-all-done.3 = f32[16,1,2,1024]{3,2,1,0:T(2,128)S(1)} async-done(((f32[16,1,2,1024]{3,2,1,0:T(2,128)}), f32[16,1,2,1024]{3,2,1,0:T(2,128)S(1)}, u32[]{:S(2)}, u32[]{:S(2)}) %all-to-all-start.3) | async-done | bytes 131104 | tf_op jit(solution)/shard_map/all_to_all | solution.py:209
  84.4 6.5 %all-to-all-start.4 = ((bf16[16,2,128,64]{2,3,1,0:T(8,128)(2,1)}), bf16[16,2,128,64]{2,3,1,0:T(8,128)(2,1)S(1)}, u32[]{:S(2)}, u32[]{:S(2)}) async-start(bf16[16,2,128,64]{2,3,1,0:T(8,128)(2,1)} %copy.118), calls=%async_computation.4 | async-start | bytes 1048576 | tf_op jit(solution)/shard_map/all_to_all | solution.py:25
  91.2 22.7 %all-to-all-done.4 = bf16[16,2,128,64]{2,3,1,0:T(8,128)(2,1)S(1)} async-done(((bf16[16,2,128,64]{2,3,1,0:T(8,128)(2,1)}), bf16[16,2,128,64]{2,3,1,0:T(8,128)(2,1)S(1)}, u32[]{:S(2)}, u32[]{:S(2)}) %all-to-all-start.4) | async-done | bytes 524320 | tf_op jit(solution)/shard_map/all_to_all | solution.py:25
  115.1 12.5 %all-to-all-start.6 = ((f32[16,2,128,64]{2,3,1,0:T(8,128)}), f32[16,2,128,64]{2,3,1,0:T(8,128)S(1)}, u32[]{:S(2)}, u32[]{:S(2)}) async-start(f32[16,2,128,64]{2,3,1,0:T(8,128)} %broadcast_in_dim.225), calls=%async_computation.6 | async-start | bytes 2097152 | tf_op jit(solution)/shard_map/all_to_all | solution.py:37
  127.6 1.4 scatter_custom_fusion.5
  129.7 43.0 %all-to-all-done.6 = f32[16,2,128,64]{2,3,1,0:T(8,128)S(1)} async-done(((f32[16,2,128,64]{2,3,1,0:T(8,128)}), f32[16,2,128,64]{2,3,1,0:T(8,128)S(1)}, u32[]{:S(2)}, u32[]{:S(2)}) %all-to-all-start.6) | async-done | bytes 1048608 | tf_op jit(solution)/shard_map/all_to_all | solution.py:37
  172.8 9.2 %all-to-all-start.5 = ((s32[32,1,8]{2,1,0:T(1,128)}), s32[32,1,8]{2,1,0:T(1,128)S(1)}, u32[]{:S(2)}, u32[]{:S(2)}) async-start(s32[32,1,8]{2,1,0:T(1,128)} %bitcast.113), calls=%async_computation.5 | async-start | bytes 32768 | tf_op jit(solution)/shard_map/all_to_all | solution.py:187
  182.8 6.2 %all-to-all-done.5 = s32[32,1,8]{2,1,0:T(1,128)S(1)} async-done(((s32[32,1,8]{2,1,0:T(1,128)}), s32[32,1,8]{2,1,0:T(1,128)S(1)}, u32[]{:S(2)}, u32[]{:S(2)}) %all-to-all-start.5) | async-done | bytes 1056 | tf_op jit(solution)/shard_map/all_to_all | solution.py:187
  189.7 7.6 %all-to-all-start.7 = ((f32[16,1,2,1024]{3,2,1,0:T(2,128)}), f32[16,1,2,1024]{3,2,1,0:T(2,128)S(1)}, u32[]{:S(2)}, u32[]{:S(2)}) async-start(f32[16,1,2,1024]{3,2,1,0:T(2,128)} %broadcast_in_dim.226), calls=%async_computation.7 | async-start | bytes 262144 | tf_op jit(solution)/shard_map/all_to_all | solution.py:37
  198.3 11.0 %all-to-all-done.7 = f32[16,1,2,1024]{3,2,1,0:T(2,128)S(1)} async-done(((f32[16,1,2,1024]{3,2,1,0:T(2,128)}), f32[16,1,2,1024]{3,2,1,0:T(2,128)S(1)}, u32[]{:S(2)}, u32[]{:S(2)}) %all-to-all-start.7) | async-done | bytes 131104 | tf_op jit(solution)/shard_map/all_to_all | solution.py:37
  210.2 9.2 %while.89 = (s32[]{:T(128)}, f32[2,128,128]{2,1,0:T(8,128)S(1)}, f32[2,6,128]{2,1,0:T(8,128)S(1)}, f32[2,6,128]{2,1,0:T(8,128)S(1)}, bf16[2,128,1024]{1,2,0:T(8,...) while((s32[]{:T(128)}, f32[2,128,128]{2,1,0:T(8,128)S(1)}, ...), condition=%wide.region_31.32_spmd, body=%wide.region_21.31_spmd.sunk | while | flops 485672448 | bytes 3947105 | solution.py:229
  212.2 1.9 fusion.332
  216.8 1.9 fusion.332
  221.0 7.2 %all-to-all-start.10 = ((f32[32,8,6]{2,1,0:T(8,128)}), f32[32,8,6]{2,1,0:T(8,128)S(1)}, u32[]{:S(2)}, u32[]{:S(2)}) async-start(f32[32,8,6]{2,1,0:T(8,128)} %bitcast_select_fusion.2), calls=%async_computation.10 | async-start | bytes 262144 | tf_op jit(solution)/shard_map/all_to_all | solution.py:243
  229.8 6.2 %all-to-all-done.10 = f32[32,8,6]{2,1,0:T(8,128)S(1)} async-done(((f32[32,8,6]{2,1,0:T(8,128)}), f32[32,8,6]{2,1,0:T(8,128)S(1)}, u32[]{:S(2)}, u32[]{:S(2)}) %all-to-all-start.10) | async-done | bytes 6176 | tf_op jit(solution)/shard_map/all_to_all | solution.py:243
  236.0 3.9 all-to-all-start.8
  242.9 4.8 %all-to-all-done.8 = f32[32,8,128]{2,1,0:T(8,128)S(1)} async-done(((f32[32,8,128]{2,1,0:T(8,128)}), f32[32,8,128]{2,1,0:T(8,128)S(1)}, u32[]{:S(2)}, u32[]{:S(2)}) %all-to-all-start.8) | async-done | bytes 131104 | tf_op jit(solution)/shard_map/all_to_all | solution.py:242
  247.6 3.9 all-to-all-start.11
  254.1 5.1 %all-to-all-done.11 = f32[32,8,6]{2,1,0:T(8,128)S(1)} async-done(((f32[32,8,6]{2,1,0:T(8,128)}), f32[32,8,6]{2,1,0:T(8,128)S(1)}, u32[]{:S(2)}, u32[]{:S(2)}) %all-to-all-start.11) | async-done | bytes 6176 | tf_op jit(solution)/shard_map/all_to_all | solution.py:189
  259.3 3.9 all-to-all-start.9
  264.5 6.2 %all-to-all-done.9 = bf16[32,8,128]{2,1,0:T(8,128)(2,1)S(1)} async-done(((bf16[32,8,128]{2,1,0:T(8,128)(2,1)}), bf16[32,8,128]{2,1,0:T(8,128)(2,1)S(1)}, u32[]{:S(2)}, u32[]{:S(2)}) %all-to-all-start.9) | async-done | bytes 65568 | tf_op jit(solution)/shard_map/all_to_all | solution.py:186
  270.6 1.4 scatter_custom_fusion.7
  273.5 5.0 %while.90 = (s32[]{:T(128)}, f32[2,128,1024]{1,2,0:T(8,128)S(1)}, f32[2,1024]{1,0:T(2,128)S(1)}, bf16[2,128,128]{2,1,0:T(8,128)(2,1)S(1)}, f32[2,6,128]{2,1,0:T(8,128)S(1)}, /*index=5*/s32[]{:T(128)}, s32[]{:T(128)}) while((s32[]{:T(128)}, f32[2,128,1024]{1,2,0:T(8,128)S(1)}, f32[2,1024]{1,0:T(2,128)S(1)}, ...), condition=%wide.region_39.40_spmd, body=%wide.region_36.39_spmd.sunk | while | flops 242777600 | bytes 1177685 | solution.py:206
  274.0 1.2 fusion.338
  278.5 15.4 %all_to_all.98 = f32[16,1,2,1024]{3,2,1,0:T(2,128)S(1)} all-to-all(f32[16,1,2,1024]{3,2,1,0:T(2,128)S(1)} %stack.45), channel_id=1, replica_groups=mesh['tile'=32,'depth'=16] {'depth'}, dimensions={0} | all-to-all | bytes 262144 | tf_op jit(solution)/shard_map/all_to_all | solution.py:209
  295.2 6.5 %all-to-all-start.13 = ((bf16[16,2,128,64]{2,3,1,0:T(8,128)(2,1)}), bf16[16,2,128,64]{2,3,1,0:T(8,128)(2,1)S(1)}, u32[]{:S(2)}, u32[]{:S(2)}) async-start(bf16[16,2,128,64]{2,3,1,0:T(8,128)(2,1)} %copy.132), calls=%async_computation.13 | async-start | bytes 1048576 | tf_op jit(solution)/shard_map/all_to_all | solution.py:25
  302.0 22.8 %all-to-all-done.13 = bf16[16,2,128,64]{2,3,1,0:T(8,128)(2,1)S(1)} async-done(((bf16[16,2,128,64]{2,3,1,0:T(8,128)(2,1)}), bf16[16,2,128,64]{2,3,1,0:T(8,128)(2,1)S(1)}, u32[]{:S(2)}, u32[]{:S(2)}) %all-to-all-start.13) | async-done | bytes 524320 | tf_op jit(solution)/shard_map/all_to_all | solution.py:25
  325.9 12.5 %all-to-all-start.14 = ((f32[16,2,128,64]{2,3,1,0:T(8,128)}), f32[16,2,128,64]{2,3,1,0:T(8,128)S(1)}, u32[]{:S(2)}, u32[]{:S(2)}) async-start(f32[16,2,128,64]{2,3,1,0:T(8,128)} %broadcast_in_dim.231), calls=%async_computation.14 | async-start | bytes 2097152 | tf_op jit(solution)/shard_map/all_to_all | solution.py:37
  338.5 45.1 %all-to-all-done.14 = f32[16,2,128,64]{2,3,1,0:T(8,128)S(1)} async-done(((f32[16,2,128,64]{2,3,1,0:T(8,128)}), f32[16,2,128,64]{2,3,1,0:T(8,128)S(1)}, u32[]{:S(2)}, u32[]{:S(2)}) %all-to-all-start.14) | async-done | bytes 1048608 | tf_op jit(solution)/shard_map/all_to_all | solution.py:37
  385.1 12.9 %all-to-all-start.15 = ((f32[16,1,2,1024]{3,2,1,0:T(2,128)}), f32[16,1,2,1024]{3,2,1,0:T(2,128)S(1)}, u32[]{:S(2)}, u32[]{:S(2)}) async-start(f32[16,1,2,1024]{3,2,1,0:T(2,128)} %broadcast_in_dim.232), calls=%async_computation.15 | async-start | bytes 262144 | tf_op jit(solution)/shard_map/all_to_all | solution.py:37
  398.8 11.1 %all-to-all-done.15 = f32[16,1,2,1024]{3,2,1,0:T(2,128)S(1)} async-done(((f32[16,1,2,1024]{3,2,1,0:T(2,128)}), f32[16,1,2,1024]{3,2,1,0:T(2,128)S(1)}, u32[]{:S(2)}, u32[]{:S(2)}) %all-to-all-start.15) | async-done | bytes 131104 | tf_op jit(solution)/shard_map/all_to_all | solution.py:37
  410.8 9.1 %while.91 = (s32[]{:T(128)}, f32[2,128,128]{2,1,0:T(8,128)S(1)}, f32[2,6,128]{2,1,0:T(8,128)S(1)}, f32[2,6,128]{2,1,0:T(8,128)S(1)}, bf16[2,128,1024]{1,2,0:T(8,...) while((s32[]{:T(128)}, f32[2,128,128]{2,1,0:T(8,128)S(1)}, ...), condition=%wide.region_55.56_spmd, body=%wide.region_45.55_spmd.sunk | while | flops 485672448 | bytes 3947105 | solution.py:229
  412.8 1.9 fusion.348
  417.4 1.9 fusion.348
  421.6 6.9 %all-to-all-start.17 = ((f32[32,8,6]{2,1,0:T(8,128)}), f32[32,8,6]{2,1,0:T(8,128)S(1)}, u32[]{:S(2)}, u32[]{:S(2)}) async-start(f32[32,8,6]{2,1,0:T(8,128)} %bitcast_select_fusion), calls=%async_computation.17 | async-start | bytes 262144 | tf_op jit(solution)/shard_map/all_to_all | solution.py:243
  429.9 6.2 %all-to-all-done.17 = f32[32,8,6]{2,1,0:T(8,128)S(1)} async-done(((f32[32,8,6]{2,1,0:T(8,128)}), f32[32,8,6]{2,1,0:T(8,128)S(1)}, u32[]{:S(2)}, u32[]{:S(2)}) %all-to-all-start.17) | async-done | bytes 6176 | tf_op jit(solution)/shard_map/all_to_all | solution.py:243
  436.2 3.9 all-to-all-start.16
  442.3 5.5 %all-to-all-done.16 = f32[32,8,128]{2,1,0:T(8,128)S(1)} async-done(((f32[32,8,128]{2,1,0:T(8,128)}), f32[32,8,128]{2,1,0:T(8,128)S(1)}, u32[]{:S(2)}, u32[]{:S(2)}) %all-to-all-start.16) | async-done | bytes 131104 | tf_op jit(solution)/shard_map/all_to_all | solution.py:242
  (293 shorter events, 65.8 us)
Async XLA Ops:
  2.2 0.6 copy-start.6
  3.6 0.6 copy-start.7
  4.2 0.7 slice-start.2
  5.0 0.7 slice-start.3
  5.8 0.7 copy-start.5
  8.6 10.5 %copy-start.4 = (f32[2,1,5,256]{3,1,2,0:T(1,128)S(1)}, f32[2,1,5,256]{3,1,2,0:T(1,128)}, u32[]{:S(2)}) copy-start(f32[2,1,5,256]{3,1,2,0:T(1,128)} %param.19) | copy-start | bytes 30724
  8.6 17.5 %all-to-all-start = ((s32[32,1,8]{2,1,0:T(1,128)}), s32[32,1,8]{2,1,0:T(1,128)S(1)}, u32[]{:S(2)}, u32[]{:S(2)}) async-start(s32[32,1,8]{2,1,0:T(1,128)} %bitcast.92), calls=%async_computation | async-start | bytes 32768 | tf_op jit(solution)/shard_map/all_to_all | solution.py:187
  19.1 0.7 copy-start.8
  21.1 0.8 copy-start.3
  26.1 12.2 %all-to-all-start.2 = ((f32[32,8,6]{2,1,0:T(8,128)}), f32[32,8,6]{2,1,0:T(8,128)S(1)}, u32[]{:S(2)}, u32[]{:S(2)}) async-start(f32[32,8,6]{2,1,0:T(8,128)} %slice_bitcast_fusion.15), calls=%async_computation.2 | async-start | bytes 262144 | tf_op jit(solution)/shard_map/all_to_all | solution.py:189
  38.2 11.4 %all-to-all-start.1 = ((bf16[32,8,128]{2,1,0:T(8,128)(2,1)}), bf16[32,8,128]{2,1,0:T(8,128)(2,1)S(1)}, u32[]{:S(2)}, u32[]{:S(2)}) async-start(bf16[32,8,128]{2,1,0:T(8,128)(2,1)} %slice_bitcast_fusion.17), calls=%async_computation.1 | async-start | bytes 131072 | tf_op jit(solution)/shard_map/all_to_all | solution.py:186
  50.8 0.6 copy-start.1
  51.4 0.8 slice-start
  57.9 25.2 %all-to-all-start.3 = ((f32[16,1,2,1024]{3,2,1,0:T(2,128)}), f32[16,1,2,1024]{3,2,1,0:T(2,128)S(1)}, u32[]{:S(2)}, u32[]{:S(2)}) async-start(f32[16,1,2,1024]{3,2,1,0:T(2,128)} %stack.44), calls=%async_computation.3 | async-start | bytes 262144 | tf_op jit(solution)/shard_map/all_to_all | solution.py:209
  83.6 7.4 %copy-start = (bf16[2,2,128,1024]{3,2,1,0:T(8,128)(2,1)S(1)}, bf16[2,2,128,1024]{3,2,1,0:T(8,128)(2,1)}, u32[]{:S(2)}) copy-start(bf16[2,2,128,1024]{3,2,1,0:T(8,128)(2,1)} %param.21) | copy-start | bytes 3145732
  84.4 29.5 %all-to-all-start.4 = ((bf16[16,2,128,64]{2,3,1,0:T(8,128)(2,1)}), bf16[16,2,128,64]{2,3,1,0:T(8,128)(2,1)S(1)}, u32[]{:S(2)}, u32[]{:S(2)}) async-start(bf16[16,2,128,64]{2,3,1,0:T(8,128)(2,1)} %copy.118), calls=%async_computation.4 | async-start | bytes 1048576 | tf_op jit(solution)/shard_map/all_to_all | solution.py:25
  115.1 57.7 %all-to-all-start.6 = ((f32[16,2,128,64]{2,3,1,0:T(8,128)}), f32[16,2,128,64]{2,3,1,0:T(8,128)S(1)}, u32[]{:S(2)}, u32[]{:S(2)}) async-start(f32[16,2,128,64]{2,3,1,0:T(8,128)} %broadcast_in_dim.225), calls=%async_computation.6 | async-start | bytes 2097152 | tf_op jit(solution)/shard_map/all_to_all | solution.py:37
  172.8 16.2 %all-to-all-start.5 = ((s32[32,1,8]{2,1,0:T(1,128)}), s32[32,1,8]{2,1,0:T(1,128)S(1)}, u32[]{:S(2)}, u32[]{:S(2)}) async-start(s32[32,1,8]{2,1,0:T(1,128)} %bitcast.113), calls=%async_computation.5 | async-start | bytes 32768 | tf_op jit(solution)/shard_map/all_to_all | solution.py:187
  189.7 19.6 %all-to-all-start.7 = ((f32[16,1,2,1024]{3,2,1,0:T(2,128)}), f32[16,1,2,1024]{3,2,1,0:T(2,128)S(1)}, u32[]{:S(2)}, u32[]{:S(2)}) async-start(f32[16,1,2,1024]{3,2,1,0:T(2,128)} %broadcast_in_dim.226), calls=%async_computation.7 | async-start | bytes 262144 | tf_op jit(solution)/shard_map/all_to_all | solution.py:37
  221.0 15.0 %all-to-all-start.10 = ((f32[32,8,6]{2,1,0:T(8,128)}), f32[32,8,6]{2,1,0:T(8,128)S(1)}, u32[]{:S(2)}, u32[]{:S(2)}) async-start(f32[32,8,6]{2,1,0:T(8,128)} %bitcast_select_fusion.2), calls=%async_computation.10 | async-start | bytes 262144 | tf_op jit(solution)/shard_map/all_to_all | solution.py:243
  236.0 11.6 %all-to-all-start.8 = ((f32[32,8,128]{2,1,0:T(8,128)}), f32[32,8,128]{2,1,0:T(8,128)S(1)}, u32[]{:S(2)}, u32[]{:S(2)}) async-start(f32[32,8,128]{2,1,0:T(8,128)} %bitcast_select_fusion.3), calls=%async_computation.8 | async-start | bytes 262144 | tf_op jit(solution)/shard_map/all_to_all | solution.py:242
  247.6 11.6 %all-to-all-start.11 = ((f32[32,8,6]{2,1,0:T(8,128)}), f32[32,8,6]{2,1,0:T(8,128)S(1)}, u32[]{:S(2)}, u32[]{:S(2)}) async-start(f32[32,8,6]{2,1,0:T(8,128)} %slice_bitcast_fusion.14), calls=%async_computation.11 | async-start | bytes 262144 | tf_op jit(solution)/shard_map/all_to_all | solution.py:189
  259.3 11.4 %all-to-all-start.9 = ((bf16[32,8,128]{2,1,0:T(8,128)(2,1)}), bf16[32,8,128]{2,1,0:T(8,128)(2,1)S(1)}, u32[]{:S(2)}, u32[]{:S(2)}) async-start(bf16[32,8,128]{2,1,0:T(8,128)(2,1)} %slice_bitcast_fusion.16), calls=%async_computation.9 | async-start | bytes 131072 | tf_op jit(solution)/shard_map/all_to_all | solution.py:186
  272.0 0.6 copy-start.2
  272.6 0.8 slice-start.1
  295.2 29.5 %all-to-all-start.13 = ((bf16[16,2,128,64]{2,3,1,0:T(8,128)(2,1)}), bf16[16,2,128,64]{2,3,1,0:T(8,128)(2,1)S(1)}, u32[]{:S(2)}, u32[]{:S(2)}) async-start(bf16[16,2,128,64]{2,3,1,0:T(8,128)(2,1)} %copy.132), calls=%async_computation.13 | async-start | bytes 1048576 | tf_op jit(solution)/shard_map/all_to_all | solution.py:25
  325.9 57.7 %all-to-all-start.14 = ((f32[16,2,128,64]{2,3,1,0:T(8,128)}), f32[16,2,128,64]{2,3,1,0:T(8,128)S(1)}, u32[]{:S(2)}, u32[]{:S(2)}) async-start(f32[16,2,128,64]{2,3,1,0:T(8,128)} %broadcast_in_dim.231), calls=%async_computation.14 | async-start | bytes 2097152 | tf_op jit(solution)/shard_map/all_to_all | solution.py:37
  385.1 24.9 %all-to-all-start.15 = ((f32[16,1,2,1024]{3,2,1,0:T(2,128)}), f32[16,1,2,1024]{3,2,1,0:T(2,128)S(1)}, u32[]{:S(2)}, u32[]{:S(2)}) async-start(f32[16,1,2,1024]{3,2,1,0:T(2,128)} %broadcast_in_dim.232), calls=%async_computation.15 | async-start | bytes 262144 | tf_op jit(solution)/shard_map/all_to_all | solution.py:37
  421.6 14.6 %all-to-all-start.17 = ((f32[32,8,6]{2,1,0:T(8,128)}), f32[32,8,6]{2,1,0:T(8,128)S(1)}, u32[]{:S(2)}, u32[]{:S(2)}) async-start(f32[32,8,6]{2,1,0:T(8,128)} %bitcast_select_fusion), calls=%async_computation.17 | async-start | bytes 262144 | tf_op jit(solution)/shard_map/all_to_all | solution.py:243
  436.2 11.6 %all-to-all-start.16 = ((f32[32,8,128]{2,1,0:T(8,128)}), f32[32,8,128]{2,1,0:T(8,128)S(1)}, u32[]{:S(2)}, u32[]{:S(2)}) async-start(f32[32,8,128]{2,1,0:T(8,128)} %bitcast_select_fusion.1), calls=%async_computation.16 | async-start | bytes 262144 | tf_op jit(solution)/shard_map/all_to_all | solution.py:242
